TPU v7x, 256 devices: a whole 4x4x8 slice. The times are simulated.
256 devices in a mesh: hist: 64 (over z, y, core), rep: 4 (over x).
Axes of the slice: x: 4, y: 4, z: 8, core: 2. Of those that a mesh axis runs over, the one named last changes fastest.
Arguments:
- features: bfloat16 [4, 16384, 512], P('rep', 'hist'), may hold values from -16 to 16
- history: bfloat16 [4, 131072, 512], P('rep', 'hist'), may hold values from -6 to 6
- blk_owner: int32 [4, 1024, 1], P('rep', 'hist'), may hold values from 0 to 63; in each aligned block of 16 rows (0 to 15, 16 to 31, ..., all dimensions but the last counted through in order) at most 2 rows name the same one
- blk_offset: int32 [4, 1024], P('rep', 'hist'), may hold values from 0 to 15
- blk_relation: int32 [4, 1024], P('rep', 'hist'), may hold values from 0 to 7
- adjacency: bfloat16 [4, 1024, 128, 128], P('rep', 'hist'), may hold values from -0.5 to 0.5
- weights: bfloat16 [9, 512, 512], replicated, may hold values from -0.09375 to 0.09375
- cotangent: bfloat16 [4, 16384, 512], P('rep', 'hist'), may hold values from -6 to 6
Outputs:
- fresh: bfloat16 [4, 16384, 512], P('rep', 'hist')
- grad_features: bfloat16 [4, 16384, 512], P('rep', 'hist')
- grad_weights: float32 [9, 262144], P(None, 'hist')
Inputs may be any that keep to these rules, and one draw needn't show every extreme that they name: `blk_owner`: within the 16 rows of one device at most 2 blocks name one owner, and in every draw some owner is named by exactly 2 rows of some device.
All inputs are finite; a program needn't handle non-finite values.
Results may differ from a plain program's by a relative error of at most 0.0053.
Values may be sent and summed in bfloat16 or wider, within the bound.
A program may use at most 128 MiB of HBM per device.

v0:
```python
import jax
import jax.numpy as jnp
from jax import lax
from jax.sharding import PartitionSpec as P


def on_device(
    features, history, blk_owner, blk_offset, blk_relation, adjacency, weights, cotangent
):
    n_hist = lax.axis_size("hist")
    owners = blk_owner.reshape(-1)
    offsets = blk_offset.reshape(-1)
    relation = blk_relation.reshape(-1)
    tiles = adjacency[0]
    nblocks = owners.shape[0]
    tile_rows = tiles.shape[-1]
    width = weights.shape[-1]
    relations = weights.shape[0] - 1
    batch_tiles = features.shape[1] // tile_rows
    per_tile = nblocks // batch_tiles
    capacity = max(2, (nblocks + n_hist - 1) // n_hist)
    matches = (owners[:, None] == jnp.arange(n_hist, dtype=jnp.int32)[None, :]).astype(jnp.int32)
    position = jnp.sum((jnp.cumsum(matches, axis=0) - matches) * matches, axis=1)
    slot_index = owners * capacity + position
    request = jnp.zeros((n_hist * capacity,), jnp.int32).at[slot_index].set(offsets)
    request = request.reshape(n_hist, capacity)
    table = history.reshape(-1, tile_rows, width)
    asked = lax.all_to_all(request, "hist", split_axis=0, concat_axis=0, tiled=True)
    arrived = lax.all_to_all(table[asked], "hist", split_axis=0, concat_axis=0, tiled=True)
    pulled = arrived.reshape(n_hist * capacity, tile_rows, width)[slot_index]
    block_sum = jnp.einsum("bij,bjd->bid", tiles, pulled, preferred_element_type=jnp.float32)
    block_sum = block_sum.reshape(batch_tiles, per_tile, tile_rows, width)
    onehot = (
        relation.reshape(batch_tiles, per_tile)[:, :, None]
        == jnp.arange(relations, dtype=jnp.int32)[None, None, :]
    ).astype(jnp.float32)
    mixed = jnp.einsum("tkr,tkid->trid", onehot, block_sum, precision=lax.Precision.HIGHEST).astype(
        jnp.bfloat16
    )
    local_x = features.reshape(batch_tiles, tile_rows, width)
    local_g = cotangent.reshape(batch_tiles, tile_rows, width)
    stacked = jnp.concatenate([local_x[:, None], mixed], axis=1)
    pre = jnp.einsum("trid,rde->tie", stacked, weights, preferred_element_type=jnp.float32)
    sigma = jax.nn.sigmoid(pre)
    fresh = (local_x.astype(jnp.float32) + pre * sigma).astype(jnp.bfloat16)
    dpre = (local_g.astype(jnp.float32) * sigma * (1.0 + pre * (1.0 - sigma))).astype(jnp.bfloat16)
    grad_x = local_g.astype(jnp.float32) + jnp.einsum(
        "tie,de->tid", dpre, weights[0], preferred_element_type=jnp.float32
    )
    grad_x = grad_x.astype(jnp.bfloat16)
    grad_w = jnp.einsum("trid,tie->rde", stacked, dpre, preferred_element_type=jnp.float32)
    flat_grad = grad_w.reshape(relations + 1, width * width)
    share = lax.psum_scatter(flat_grad, "hist", scatter_dimension=1, tiled=True)
    summed = lax.psum(share, "rep")
    fresh = fresh.reshape(1, batch_tiles * tile_rows, width)
    grad_x = grad_x.reshape(1, batch_tiles * tile_rows, width)
    return (fresh, grad_x, summed)


def solution(mesh):
    in_specs = (
        P("rep", "hist", None),
        P("rep", "hist", None),
        P("rep", "hist", None),
        P("rep", "hist"),
        P("rep", "hist"),
        P("rep", "hist", None, None),
        P(),
        P("rep", "hist", None),
    )
    out_specs = (P("rep", "hist", None), P("rep", "hist", None), P(None, "hist"))
    return jax.shard_map(
        on_device, mesh=mesh, in_specs=in_specs, out_specs=out_specs, check_vma=False
    )
```

profile of v0, /device:TPU:8, one launch (start us, length us, event | category | flops | bytes accessed | tf_op | source)
XLA Modules:
  0.0 727.3 jit_solution(9442419736519274689)
XLA Ops:
  7.2 0.9 fusion.18
  8.1 0.8 select_reduce_fusion
  8.9 0.7 fusion.22
  9.6 0.8 scatter_custom_fusion
  10.4 0.1 all_to_all.11
  10.5 20.5 %all_to_all.17 = s32[64,1,2]{2,1,0:T(1,128)S(1)} all-to-all(s32[64,1,2]{2,1,0:T(1,128)S(1)} %bitcast.70), channel_id=1, replica_groups=mesh['hist'=64,'rep'=4] {'hist'}, dimensions={0} | all-to-all | bytes 1024 | tf_op jit(solution)/shard_map/all_to_all | solution.py:28
  31.0 0.1 copy.24
  31.1 0.1 copy.25
  31.2 0.1 reshape.107
  31.3 7.8 %gather_fusion = bf16[128,128,512]{2,1,0:T(8,128)(2,1)} fusion(bf16[16,128,512]{2,1,0:T(8,128)(2,1)S(1)} %bitcast.61, s32[1024]{0:T(1024)S(1)} %pad_clamp_fusion.1), kind=kCustom, calls=%fused_computation | custom fusion | bytes 33554944 | tf_op jit(solution)/shard_map/gather | solution.py:29
  39.1 6.8 all-to-all-start.1
  45.9 0.0 reduce-scatter.2.cloned.1.call-start
  46.0 0.5 broadcast.78
  46.5 0.7 reduce.3
  47.2 0.1 eq.30
  47.3 0.4 copy.28
  47.7 368.5 %all-to-all-done.1 = bf16[64,2,128,512]{3,2,1,0:T(8,128)(2,1)} async-done(((bf16[64,2,128,512]{3,2,1,0:T(8,128)(2,1)}), bf16[64,2,128,512]{3,2,1,0:T(8,128)(2,1)}, u32[]{:S(2)}, u32[]{:S(2)}) %all-to-all-start.1) | async-done | bytes 16777248 | tf_op jit(solution)/shard_map/all_to_all | solution.py:29
  416.2 6.4 gather_fusion.1
  422.6 2.7 fusion.14
  425.3 5.5 copy.27
  430.8 4.3 convolution_convert_fusion
  435.2 2.0 pad_maximum_fusion
  437.2 6.1 fusion.12
  443.3 9.4 %convolution_bitcast_fusion = f32[9,512,512]{2,1,0:T(8,128)} fusion(bf16[2,9,128,512]{3,1,2,0:T(8,128)(2,1)S(1)} %pad_maximum_fusion, bf16[2,128,512]{2,1,0:T(8,128)(2,1)S(1)} %bitcast.68, f32[2,128,512]{2,1,0:T(8,128)S(1)} %get-tuple-element.4), kind=kOutput, calls=%fused_computation.6 | convolution fusion | flops 1209270272 | bytes 12582912 | tf_op jit(solution)/shard_map/trid,tie->rde/dot_general | solution.py:51
  452.7 11.5 %pad.4 = f32[16,512,512]{2,1,0:T(8,128)} pad(f32[9,512,512]{2,1,0:T(8,128)} %convolution_bitcast_fusion, f32[]{:T(128)} %constant.34), padding=0_7x0_0x0_0 | pad | bytes 26214404
  464.3 17.7 %copy.35 = f32[2,8,512,512]{3,1,2,0:T(8,128)} copy(f32[2,8,512,512]{3,2,1,0:T(8,128)} %bitcast.64) | data formatting | bytes 33554432
  482.0 0.0 reduce-scatter.2.cloned.1.call-update
  482.0 0.0 all-reduce.2.cloned.1.call-start
  482.1 188.4 %reduce-scatter.2.cloned.1.call-done = f32[9,4096]{1,0:T(8,128)} async-done(((f32[9,262144]{1,0:T(8,128)}), f32[9,4096]{1,0:T(8,128)}) %reduce-scatter.2.cloned.1.call-update) | async-done | bytes 147472 | tf_op jit(solution)/shard_map/reduce_scatter | solution.py:53
  670.5 2.1 fusion.9
  672.6 46.2 %all-reduce.2.cloned.1.call-done = f32[9,4096]{1,0:T(8,128)} async-done(((f32[9,4096]{1,0:T(8,128)}), f32[9,4096]{1,0:T(8,128)}) %all-reduce.2.cloned.1.call-update) | async-done | bytes 147472 | tf_op jit(solution)/shard_map/psum | solution.py:54
  718.8 1.7 copy.45
  (17 shorter events, 0.1 us)
Async XLA Ops:
  7.2 24.2 %copy-start = (bf16[1,2048,512]{2,1,0:T(8,128)(2,1)S(1)}, bf16[1,2048,512]{2,1,0:T(8,128)(2,1)}, u32[]{:S(2)}) copy-start(bf16[1,2048,512]{2,1,0:T(8,128)(2,1)} %param.9) | copy-start | bytes 6291460
  39.1 7.4 %copy-start.5 = (s32[1,16]{1,0:T(1,128)S(1)}, s32[1,16]{1,0:T(1,128)}, u32[]{:S(2)}) copy-start(s32[1,16]{1,0:T(1,128)} %param.12) | copy-start | bytes 196
  39.1 8.1 %copy-start.3 = (bf16[1,256,512]{2,1,0:T(8,128)(2,1)S(1)}, bf16[1,256,512]{2,1,0:T(8,128)(2,1)}, u32[]{:S(2)}) copy-start(bf16[1,256,512]{2,1,0:T(8,128)(2,1)} %param.8) | copy-start | bytes 786436
  39.1 377.1 %all-to-all-start.1 = ((bf16[64,2,128,512]{3,2,1,0:T(8,128)(2,1)}), bf16[64,2,128,512]{3,2,1,0:T(8,128)(2,1)}, u32[]{:S(2)}, u32[]{:S(2)}) async-start(bf16[64,2,128,512]{3,2,1,0:T(8,128)(2,1)} %bitcast.62), calls=%async_computation.1 | async-start | bytes 33554432 | tf_op jit(solution)/shard_map/all_to_all | solution.py:29
  45.9 376.7 %copy-start.2 = (bf16[1,16,128,128]{3,2,1,0:T(8,128)(2,1)S(1)}, bf16[1,16,128,128]{3,2,1,0:T(8,128)(2,1)}, u32[]{:S(2)}) copy-start(bf16[1,16,128,128]{3,2,1,0:T(8,128)(2,1)} %param.13) | copy-start | bytes 1572868
  45.9 624.5 %reduce-scatter.2.cloned.1.call-start = ((), (), s32[]{:S(2)}) async-start(), calls=%async_computation.3 | async-start | bytes 17039360 | tf_op jit(solution)/shard_map/reduce_scatter | solution.py:53
  437.2 6.1 copy-start.4
  482.0 238.5 %copy-start.1 = (bf16[1,2048,512]{2,1,0:T(8,128)(2,1)S(1)}, bf16[1,2048,512]{2,1,0:T(8,128)(2,1)}, u32[]{:S(2)}) copy-start(bf16[1,2048,512]{2,1,0:T(8,128)(2,1)} %param.9) | copy-start | bytes 6291460
  482.0 236.8 %all-reduce.2.cloned.1.call-start = ((), (), s32[]{:S(2)}) async-start(), calls=%async_computation.4 | async-start | bytes 524288 | tf_op jit(solution)/shard_map/psum | solution.py:54
Sparse Core Ops, SparseCore 0:
  482.1 188.3 reduce-scatter.1
  672.8 45.9 all-reduce.1
where the time goes:
time: 728 us; the launch traced here: 727 us
  waiting for transfers between devices  603 us (83%)
  local copies, waits for them, and re-layouts  52.9 us (7%)
  matrix products  24.7 us (3%)
  blocking collectives  20.5 us (3%)
  between operations  14.2 us (2%)
    all_to_all x1, waiting for transfers between devices, on_device(): lax.all_to_all(table[asked], 'hist', split_axis=0, concat_axis=0, tiled=T...  368 us
    reduce_scatter x1, waiting for transfers between devices, on_device(): share = lax.psum_scatter(flat_grad, 'hist', scatter_dimension=1, tiled=True)  188 us
    psum x1, waiting for transfers between devices, on_device(): summed = lax.psum(share, 'rep')  46.2 us
    unnamed x16, local copies, waits for them, and re-layouts  31.5 us
    all_to_all x1, blocking collectives, on_device(): lax.all_to_all(request, 'hist', split_axis=0, concat_axis=0, tiled=True)  20.5 us
  transfers between devices with their start and end apart: 3, of which 3 were waited for; matrix products, arithmetic and copies ran while one was open for 1% of the time, Pallas kernels for 0%

commit v1 on v0

--- a/solution.py
+++ b/solution.py
@@ -51,7 +51,7 @@
     grad_w = jnp.einsum("trid,tie->rde", stacked, dpre, preferred_element_type=jnp.float32)
     flat_grad = grad_w.reshape(relations + 1, width * width)
     share = lax.psum_scatter(flat_grad, "hist", scatter_dimension=1, tiled=True)
-    summed = lax.psum(share, "rep")
+    summed = jnp.sum(lax.all_gather(share, "rep"), axis=0)
     fresh = fresh.reshape(1, batch_tiles * tile_rows, width)
     grad_x = grad_x.reshape(1, batch_tiles * tile_rows, width)
     return (fresh, grad_x, summed)

time: 728 us -> 695 us (0.955)
  waiting for transfers between devices: 603 us -> 555 us
  blocking collectives: 20.5 us -> 36.1 us
    psum x1 -> x0, waiting for transfers between devices: 46.2 us -> none  [on_device(): summed = lax.psum(share, 'rep')]
    all_gather x0 -> x1, blocking collectives: none -> 15.6 us  [on_device(): summed = jnp.sum(lax.all_gather(share, 'rep'), axis=0)]
    unnamed x16 -> x15, local copies, waits for them, and re-layouts: 31.5 us -> 29.8 us
  transfers between devices with their start and end apart: 3 -> 2, of which waited for: 3 -> 2; matrix products, arithmetic and copies ran while one was open for 1% -> 1% of each run, Pallas kernels for 0% -> 0%
where the time goes in v1:
time: 695 us; the launch traced here: 694 us
  waiting for transfers between devices  555 us (80%)
  local copies, waits for them, and re-layouts  51.2 us (7%)
  blocking collectives  36.1 us (5%)
  matrix products  24.8 us (4%)
  between operations  14.2 us (2%)
    all_to_all x1, waiting for transfers between devices, on_device(): lax.all_to_all(table[asked], 'hist', split_axis=0, concat_axis=0, tiled=T...  368 us
    reduce_scatter x1, waiting for transfers between devices, on_device(): share = lax.psum_scatter(flat_grad, 'hist', scatter_dimension=1, tiled=True)  186 us
    unnamed x15, local copies, waits for them, and re-layouts  29.8 us
    all_to_all x1, blocking collectives, on_device(): lax.all_to_all(request, 'hist', split_axis=0, concat_axis=0, tiled=True)  20.5 us
    all_gather x1, blocking collectives, on_device(): summed = jnp.sum(lax.all_gather(share, 'rep'), axis=0)  15.6 us
  transfers between devices with their start and end apart: 2, of which 2 were waited for; matrix products, arithmetic and copies ran while one was open for 1% of the time, Pallas kernels for 0%

profile of v1, /device:TPU:8, one launch (start us, length us, event | category | flops | bytes accessed | tf_op | source)
XLA Modules:
  0.0 693.7 jit_solution(17594774626456065872)
XLA Ops:
  7.2 0.0 copy-start
  7.2 0.9 fusion.18
  8.1 0.8 select_reduce_fusion
  8.9 0.7 fusion.22
  9.6 0.8 scatter_custom_fusion
  10.4 0.1 all_to_all.11
  10.5 20.5 %all_to_all.17 = s32[64,1,2]{2,1,0:T(1,128)S(1)} all-to-all(s32[64,1,2]{2,1,0:T(1,128)S(1)} %bitcast.72), channel_id=1, replica_groups=mesh['hist'=64,'rep'=4] {'hist'}, dimensions={0} | all-to-all | bytes 1024 | tf_op jit(solution)/shard_map/all_to_all | solution.py:28
  31.0 0.1 copy.24
  31.1 0.1 copy.25
  31.2 0.1 reshape.107
  31.3 7.8 %gather_fusion = bf16[128,128,512]{2,1,0:T(8,128)(2,1)} fusion(bf16[16,128,512]{2,1,0:T(8,128)(2,1)S(1)} %bitcast.62, s32[1024]{0:T(1024)S(1)} %pad_clamp_fusion.1), kind=kCustom, calls=%fused_computation | custom fusion | bytes 33554944 | tf_op jit(solution)/shard_map/gather | solution.py:29
  39.1 6.8 all-to-all-start.1
  45.9 0.0 reduce-scatter.2.cloned.1.call-start
  46.0 0.5 broadcast.78
  46.5 0.7 reduce.4
  47.2 0.1 eq.30
  47.3 0.4 copy.28
  47.7 368.5 %all-to-all-done.1 = bf16[64,2,128,512]{3,2,1,0:T(8,128)(2,1)} async-done(((bf16[64,2,128,512]{3,2,1,0:T(8,128)(2,1)}), bf16[64,2,128,512]{3,2,1,0:T(8,128)(2,1)}, u32[]{:S(2)}, u32[]{:S(2)}) %all-to-all-start.1) | async-done | bytes 16777248 | tf_op jit(solution)/shard_map/all_to_all | solution.py:29
  416.2 6.4 gather_fusion.1
  422.6 2.7 fusion.14
  425.3 5.5 copy.27
  430.8 4.3 convolution_convert_fusion
  435.2 2.0 pad_maximum_fusion
  437.2 6.1 fusion.12
  443.3 9.4 %convolution_bitcast_fusion = f32[9,512,512]{2,1,0:T(8,128)} fusion(bf16[2,9,128,512]{3,1,2,0:T(8,128)(2,1)S(1)} %pad_maximum_fusion, bf16[2,128,512]{2,1,0:T(8,128)(2,1)S(1)} %bitcast.69, f32[2,128,512]{2,1,0:T(8,128)S(1)} %get-tuple-element.4), kind=kOutput, calls=%fused_computation.6 | convolution fusion | flops 1209270272 | bytes 12582912 | tf_op jit(solution)/shard_map/trid,tie->rde/dot_general | solution.py:51
  452.7 11.5 %pad.4 = f32[16,512,512]{2,1,0:T(8,128)} pad(f32[9,512,512]{2,1,0:T(8,128)} %convolution_bitcast_fusion, f32[]{:T(128)} %constant.4.clone.1), padding=0_7x0_0x0_0 | pad | bytes 26214404
  464.3 17.7 %copy.35 = f32[2,8,512,512]{3,1,2,0:T(8,128)} copy(f32[2,8,512,512]{3,2,1,0:T(8,128)} %bitcast.65) | data formatting | bytes 33554432
  482.0 0.0 reduce-scatter.2.cloned.1.call-update
  482.0 2.3 fusion.9
  484.3 186.2 %reduce-scatter.2.cloned.1.call-done = f32[9,4096]{1,0:T(8,128)} async-done(((f32[9,262144]{1,0:T(8,128)}), f32[9,4096]{1,0:T(8,128)}) %reduce-scatter.2.cloned.1.call-update) | async-done | bytes 147472 | tf_op jit(solution)/shard_map/reduce_scatter | solution.py:53
  670.5 15.6 %all-gather.1 = f32[4,9,4096]{2,1,0:T(8,128)S(1)} all-gather(f32[1,9,4096]{2,1,0:T(8,128)} %bitcast.71), channel_id=2, replica_groups=mesh['hist'=64,'rep'=4] {'rep'}, dimensions={0}, use_global_device_ids=true | all-gather | bytes 737280 | tf_op jit(solution)/shard_map/all_gather | solution.py:54
  686.1 0.8 reduce_sum.22
  (15 shorter events, 0.1 us)
Async XLA Ops:
  7.2 24.2 %copy-start = (bf16[1,2048,512]{2,1,0:T(8,128)(2,1)S(1)}, bf16[1,2048,512]{2,1,0:T(8,128)(2,1)}, u32[]{:S(2)}) copy-start(bf16[1,2048,512]{2,1,0:T(8,128)(2,1)} %param.9) | copy-start | bytes 6291460
  39.1 7.4 %copy-start.5 = (s32[1,16]{1,0:T(1,128)S(1)}, s32[1,16]{1,0:T(1,128)}, u32[]{:S(2)}) copy-start(s32[1,16]{1,0:T(1,128)} %param.12) | copy-start | bytes 196
  39.1 8.1 %copy-start.3 = (bf16[1,256,512]{2,1,0:T(8,128)(2,1)S(1)}, bf16[1,256,512]{2,1,0:T(8,128)(2,1)}, u32[]{:S(2)}) copy-start(bf16[1,256,512]{2,1,0:T(8,128)(2,1)} %param.8) | copy-start | bytes 786436
  39.1 377.1 %all-to-all-start.1 = ((bf16[64,2,128,512]{3,2,1,0:T(8,128)(2,1)}), bf16[64,2,128,512]{3,2,1,0:T(8,128)(2,1)}, u32[]{:S(2)}, u32[]{:S(2)}) async-start(bf16[64,2,128,512]{3,2,1,0:T(8,128)(2,1)} %bitcast.63), calls=%async_computation.1 | async-start | bytes 33554432 | tf_op jit(solution)/shard_map/all_to_all | solution.py:29
  45.9 376.7 %copy-start.2 = (bf16[1,16,128,128]{3,2,1,0:T(8,128)(2,1)S(1)}, bf16[1,16,128,128]{3,2,1,0:T(8,128)(2,1)}, u32[]{:S(2)}) copy-start(bf16[1,16,128,128]{3,2,1,0:T(8,128)(2,1)} %param.13) | copy-start | bytes 1572868
  45.9 624.5 %reduce-scatter.2.cloned.1.call-start = ((), (), s32[]{:S(2)}) async-start(), calls=%async_computation.3 | async-start | bytes 17039360 | tf_op jit(solution)/shard_map/reduce_scatter | solution.py:53
  437.2 6.1 copy-start.4
  482.0 204.9 %copy-start.1 = (bf16[1,2048,512]{2,1,0:T(8,128)(2,1)S(1)}, bf16[1,2048,512]{2,1,0:T(8,128)(2,1)}, u32[]{:S(2)}) copy-start(bf16[1,2048,512]{2,1,0:T(8,128)(2,1)} %param.9) | copy-start | bytes 6291460
Sparse Core Ops, SparseCore 0:
  482.1 188.3 reduce-scatter.1
